TPU v7x, 256 devices: a whole 4x4x8 slice. The times are simulated.
256 devices in a mesh: prow: 16 (over y, x), pcol: 16 (over z, core).
Axes of the slice: x: 4, y: 4, z: 8, core: 2. Of those that a mesh axis runs over, the one named last changes fastest.
Arguments:
- matrix: bfloat16 [1, 8192, 1, 8192], P(None, 'prow', None, 'pcol'), may hold values from -8 to 300, as said below
Outputs:
- factored: bfloat16 [1, 8192, 1, 8192], P(None, 'prow', None, 'pcol')
Inputs may be any that keep to these rules, and one draw needn't show every extreme that they name: `matrix`: every leading 512 x 512 diagonal block met by the steps has an LU factorization without pivoting, with pivots far from zero.
All inputs are finite; a program needn't handle non-finite values.
Results may differ from a plain program's by a relative error of at most 0.002.
Values may be sent and summed in bfloat16 or wider, within the bound.
A program may use at most 64 MiB of HBM per device.

v0:
```python
import jax
import jax.numpy as jnp
from jax import lax
from jax.sharding import PartitionSpec as P


def from_root(shard, axis, root):
    mine = lax.axis_index(axis) == root
    return lax.psum(jnp.where(mine, shard, jnp.zeros_like(shard)), axis)


def high_dot(left, right):
    return jnp.dot(left, right, precision=lax.Precision.HIGHEST)


def lu_loop(block):
    size = block.shape[0]
    index = jnp.arange(size)

    def one_column(col, work):
        column = lax.dynamic_slice_in_dim(work, col, 1, 1)[:, 0]
        row_line = lax.dynamic_slice_in_dim(work, col, 1, 0)[0]
        pivot = jnp.sum(jnp.where(index == col, column, jnp.zeros_like(column)))
        under = index > col
        below = jnp.where(under, column / pivot, jnp.zeros_like(column))
        right = jnp.where(under, row_line, jnp.zeros_like(row_line))
        work = work - below[:, None] * right[None, :]
        target = jnp.logical_and(under[:, None], (index == col)[None, :])
        return jnp.where(target, below[:, None], work)

    return lax.fori_loop(0, size, one_column, block)


def nilpotent_inverse(strict):
    size = strict.shape[0]
    ident = jnp.eye(size, dtype=strict.dtype)
    power = -strict
    result = ident + power
    for level in range(1, max((size - 1).bit_length(), 1)):
        power = high_dot(power, power)
        result = high_dot(result, ident + power)
    return result


def base_parts(block):
    packed = lu_loop(block)
    size = block.shape[0]
    ident = jnp.eye(size, dtype=packed.dtype)
    l_inverse = nilpotent_inverse(jnp.tril(packed, -1))
    upper = jnp.triu(packed)
    pivots = jnp.sum(upper * ident, axis=1)
    scaled = upper / pivots[:, None]
    u_inverse = nilpotent_inverse(scaled - ident) / pivots[None, :]
    return (packed, l_inverse, u_inverse)


def blocked_lu(block):
    size = block.shape[0]
    if size <= 64:
        return base_parts(block)
    half = size // 2
    top_packed, top_linv, top_uinv = blocked_lu(block[:half, :half])
    top_right = high_dot(top_linv, block[:half, half:])
    bottom_left = high_dot(block[half:, :half], top_uinv)
    schur = block[half:, half:] - high_dot(bottom_left, top_right)
    low_packed, low_linv, low_uinv = blocked_lu(schur)
    zeros_half = jnp.zeros((half, half), block.dtype)
    upper_rows = jnp.concatenate([top_packed, top_right], axis=1)
    lower_rows = jnp.concatenate([bottom_left, low_packed], axis=1)
    packed = jnp.concatenate([upper_rows, lower_rows], axis=0)
    l_corner = -high_dot(high_dot(low_linv, bottom_left), top_linv)
    l_inverse = jnp.concatenate(
        [
            jnp.concatenate([top_linv, zeros_half], axis=1),
            jnp.concatenate([l_corner, low_linv], axis=1),
        ],
        axis=0,
    )
    u_corner = -high_dot(high_dot(top_uinv, top_right), low_uinv)
    u_inverse = jnp.concatenate(
        [
            jnp.concatenate([top_uinv, u_corner], axis=1),
            jnp.concatenate([zeros_half, low_uinv], axis=1),
        ],
        axis=0,
    )
    return (packed, l_inverse, u_inverse)


def factor_parts(diag_bf):
    packed, l_inverse, u_inverse = blocked_lu(diag_bf.astype(jnp.float32))
    return (packed.astype(jnp.bfloat16), l_inverse, u_inverse)


def solve_column(column, u_inverse):
    return jnp.einsum(
        "anb,bc->anc", column.astype(jnp.float32), u_inverse, precision=lax.Precision.HIGHEST
    ).astype(jnp.bfloat16)


def solve_row(row_panel, l_inverse):
    return jnp.einsum(
        "ab,bcd->acd", l_inverse, row_panel.astype(jnp.float32), precision=lax.Precision.HIGHEST
    ).astype(jnp.bfloat16)


def per_device(matrix):
    row_count = matrix.shape[0]
    col_count = matrix.shape[2]
    n_rows = lax.axis_size("prow")
    n_cols = lax.axis_size("pcol")
    my_row = lax.axis_index("prow")
    my_col = lax.axis_index("pcol")
    row_global = jnp.arange(row_count) * n_rows + my_row
    col_global = jnp.arange(col_count) * n_cols + my_col
    columns = [matrix[:, :, 0, :]]
    owner_row = 0 % n_rows
    owner_col = 0 % n_cols
    local_row = 0 // n_rows
    local_col = 0 // n_cols
    diag_raw = columns[local_col][local_row]
    col_raw = columns[local_col]
    row_raw = jnp.stack([piece[local_row] for piece in columns], axis=1)
    below = (row_global > 0)[:, None, None]
    right = (col_global > 0)[None, :, None]
    diag_every = from_root(diag_raw, ("prow", "pcol"), owner_row * n_cols + owner_col)
    packed_col, l_inverse, u_inverse = factor_parts(diag_every)
    l_solved = solve_column(col_raw, u_inverse)
    l_send = jnp.where(below, l_solved, jnp.zeros_like(l_solved))
    l_all = from_root(l_send, "pcol", owner_col)
    u_solved = solve_row(row_raw, l_inverse)
    u_send = jnp.where(right, u_solved, jnp.zeros_like(u_solved))
    u_all = from_root(u_send, "prow", owner_row)
    product = jnp.einsum("anb,bcd->ancd", l_all, u_all, preferred_element_type=jnp.float32)
    piece = (columns[0].astype(jnp.float32) - product[:, :, 0, :]).astype(jnp.bfloat16)
    at_diag = (row_global == 0)[:, None, None]
    panel_values = jnp.where(below, l_solved, jnp.where(at_diag, packed_col[None, :, :], piece))
    piece = jnp.where(my_col == owner_col, panel_values, piece)
    glob = col_global[0]
    row_values = jnp.where(
        glob > 0, u_solved[:, 0, :], jnp.where(glob == 0, packed_col, piece[local_row])
    )
    piece = piece.at[local_row].set(jnp.where(my_row == owner_row, row_values, piece[local_row]))
    updated = [piece]
    return jnp.stack(updated, axis=2)


def solution(mesh):
    placed = (P(None, "prow", None, "pcol"),)
    return jax.shard_map(
        per_device,
        mesh=mesh,
        in_specs=placed,
        out_specs=P(None, "prow", None, "pcol"),
        check_vma=False,
    )
```

profile of v0, /device:TPU:40, one launch (start us, length us, event | category | flops | bytes accessed | tf_op | source)
XLA Modules:
  0.0 1295.9 jit_solution(6632582190497265830)
XLA Ops:
  6.5 1.9 bitcast_select_fusion.24
  8.5 259.8 %all-reduce.18.cloned.1.call-done = bf16[512,512]{1,0:T(8,128)(2,1)} async-done(((bf16[512,512]{1,0:T(8,128)(2,1)}), bf16[512,512]{1,0:T(8,128)(2,1)}) %all-reduce.18.cloned.1.call-update) | async-done | bytes 524304 | tf_op jit(solution)/shard_map/psum | solution.py:9
  268.3 0.7 slice.135
  269.1 94.8 %while.121 = (s32[]{:T(128)}, f32[64,64]{0,1:T(8,128)S(1)}, s32[]{:T(128)}) while((s32[]{:T(128)}, f32[64,64]{0,1:T(8,128)S(1)}, s32[]{:T(128)}) %tuple.291), condition=%wide.region_3.4_spmd.clone.clone, body=%wide.region_1.3_spmd.clone.clone.sunk | while | flops 17025 | bytes 70721 | solution.py:31
  269.7 0.7 fusion.688
  272.7 0.7 fusion.688
  274.2 0.7 fusion.688
  277.1 0.7 fusion.688
  278.6 0.7 fusion.688
  281.6 0.7 fusion.688
  283.1 0.7 fusion.688
  287.5 0.7 fusion.688
  368.8 94.8 %while.122 = (s32[]{:T(128)}, f32[64,64]{0,1:T(8,128)S(1)}, s32[]{:T(128)}) while((s32[]{:T(128)}, f32[64,64]{0,1:T(8,128)S(1)}, s32[]{:T(128)}) %tuple.294), condition=%wide.region_7.8_spmd.clone.clone, body=%wide.region_5.7_spmd.clone.clone.sunk | while | flops 17025 | bytes 70721 | solution.py:31
  469.5 94.8 %while.123 = (s32[]{:T(128)}, f32[64,64]{0,1:T(8,128)S(1)}, s32[]{:T(128)}) while((s32[]{:T(128)}, f32[64,64]{0,1:T(8,128)S(1)}, s32[]{:T(128)}) %tuple.297), condition=%wide.region_11.12_spmd.clone.clone, body=%wide.region_9.11_spmd.clone.clone.sunk | while | flops 17025 | bytes 70721 | solution.py:31
  569.1 94.8 %while.124 = (s32[]{:T(128)}, f32[64,64]{0,1:T(8,128)S(1)}, s32[]{:T(128)}) while((s32[]{:T(128)}, f32[64,64]{0,1:T(8,128)S(1)}, s32[]{:T(128)}) %tuple.300), condition=%wide.region_15.16_spmd.clone.clone, body=%wide.region_13.15_spmd.clone.clone.sunk | while | flops 17025 | bytes 70721 | solution.py:31
  670.7 94.8 %while.125 = (s32[]{:T(128)}, f32[64,64]{0,1:T(8,128)S(1)}, s32[]{:T(128)}) while((s32[]{:T(128)}, f32[64,64]{0,1:T(8,128)S(1)}, s32[]{:T(128)}) %tuple.303), condition=%wide.region_19.20_spmd.clone.clone, body=%wide.region_17.19_spmd.clone.clone.sunk | while | flops 17025 | bytes 70721 | solution.py:31
  770.2 94.9 %while.126 = (s32[]{:T(128)}, f32[64,64]{0,1:T(8,128)S(1)}, s32[]{:T(128)}) while((s32[]{:T(128)}, f32[64,64]{0,1:T(8,128)S(1)}, s32[]{:T(128)}) %tuple.306), condition=%wide.region_23.24_spmd.clone.clone, body=%wide.region_21.23_spmd.clone.clone.sunk | while | flops 17025 | bytes 70721 | solution.py:31
  871.2 94.8 %while.127 = (s32[]{:T(128)}, f32[64,64]{0,1:T(8,128)S(1)}, s32[]{:T(128)}) while((s32[]{:T(128)}, f32[64,64]{0,1:T(8,128)S(1)}, s32[]{:T(128)}) %tuple.309), condition=%wide.region_27.28_spmd.clone.clone, body=%wide.region_25.27_spmd.clone.clone.sunk | while | flops 17025 | bytes 70721 | solution.py:31
  970.8 94.8 %while.128 = (s32[]{:T(128)}, f32[64,64]{0,1:T(8,128)S(1)}, s32[]{:T(128)}) while((s32[]{:T(128)}, f32[64,64]{0,1:T(8,128)S(1)}, s32[]{:T(128)}) %tuple.312), condition=%wide.region_31.32_spmd.clone.clone, body=%wide.region_29.31_spmd.clone.clone.sunk | while | flops 17025 | bytes 70721 | solution.py:31
  1073.4 2.1 select_select_fusion.1
  1075.5 1.8 select_select_fusion
  1078.0 106.9 %all-reduce.20.cloned.1.call-done = bf16[512,512]{1,0:T(8,128)(2,1)} async-done(((bf16[512,512]{1,0:T(8,128)(2,1)}), bf16[512,512]{1,0:T(8,128)(2,1)}) %all-reduce.20.cloned.1.call-update) | async-done | bytes 524304 | tf_op jit(solution)/shard_map/psum | solution.py:9
  1185.0 101.7 %all-reduce.22.cloned.1.call-done = bf16[512,512]{1,0:T(8,128)(2,1)} async-done(((bf16[512,512]{1,0:T(8,128)(2,1)}), bf16[512,512]{1,0:T(8,128)(2,1)}) %all-reduce.22.cloned.1.call-update) | async-done | bytes 524304 | tf_op jit(solution)/shard_map/psum | solution.py:9
  1286.7 2.7 select_bitcast_fusion
  (3332 shorter events, 775.1 us)
Async XLA Ops:
  6.5 261.8 %all-reduce.18.cloned.1.call-start = ((), (), s32[]{:S(2)}) async-start(), calls=%async_computation | async-start | bytes 1048576 | tf_op jit(solution)/shard_map/psum | solution.py:9
  8.4 1176.5 %all-reduce.20.cloned.1.call-start = ((), (), s32[]{:S(2)}) async-start(), calls=%async_computation.1 | async-start | bytes 1048576 | tf_op jit(solution)/shard_map/psum | solution.py:9
  366.0 1.9 copy-start
  1072.3 1.0 copy-start.1
  1075.5 211.2 %all-reduce.22.cloned.1.call-start = ((), (), s32[]{:S(2)}) async-start(), calls=%async_computation.2 | async-start | bytes 1048576 | tf_op jit(solution)/shard_map/psum | solution.py:9
  1077.6 209.1 %copy-start.2 = (bf16[512,512]{1,0:T(8,128)(2,1)S(1)}, bf16[512,512]{1,0:T(8,128)(2,1)}, u32[]{:S(2)}) copy-start(bf16[512,512]{1,0:T(8,128)(2,1)} %get-tuple-element.770) | copy-start | bytes 1572868
Sparse Core Ops, SparseCore 0:
  12.8 255.4 all-reduce.17
  1075.6 109.3 all-reduce.19
  1188.2 98.4 all-reduce.21
where the time goes:
time: 1300 us
  other arithmetic  701 us (54%)
  waiting for transfers between devices  469 us (36%)
  matrix products  46.8 us (4%)
  local copies, waits for them, and re-layouts  41.4 us (3%)
  loops' own time  23 us (2%)
  between operations  15 us (1%)
    psum x3, waiting for transfers between devices, from_root(): return lax.psum(jnp.where(mine, shard, jnp.zeros_like(shard)), axis)  468 us
    broadcast_in_dim x512, other arithmetic, one_column(): return jnp.where(target, below[:, None], work)  335 us
    reduce_sum x512, other arithmetic, one_column(): pivot = jnp.sum(jnp.where(index == col, column, jnp.zeros_like(column)))  310 us
    select_n x512, other arithmetic, one_column(): return jnp.where(target, below[:, None], work)  43.5 us
    dot_general x209, matrix products, high_dot(): return jnp.dot(left, right, precision=lax.Precision.HIGHEST)  40.2 us
    while x512, local copies, waits for them, and re-layouts  38 us
  transfers between devices with their start and end apart: 3, of which 3 were waited for; matrix products, arithmetic and copies ran while one was open for 0% of the time, Pallas kernels for 0%

commit v1 on v0

v1 whole, which is shorter than its diff:
```python
import functools

import jax
import jax.numpy as jnp
from jax import lax
from jax.experimental import pallas as pl
from jax.experimental.pallas import tpu as pltpu
from jax.sharding import PartitionSpec as P

F32 = jnp.float32
BF = jnp.bfloat16
NB = 512
HB = 256
TB = 128
MESH = pl.DeviceIdType.MESH


def split(x):
    hi = x.astype(BF)
    lo = (x - hi.astype(F32)).astype(BF)
    return hi, lo

def dot(a, b):
    return jnp.dot(a, b, preferred_element_type=F32)

def dot3s(a, b):
    ah, al = a; bh, bl = b
    return dot(jnp.concatenate([ah, al, ah], 1), jnp.concatenate([bh, bh, bl], 0))

def dot3(a, b):
    return dot3s(split(a), split(b))

def iotas(rows=8):
    return (lax.broadcasted_iota(jnp.int32, (rows, 128), 0), lax.broadcasted_iota(jnp.int32, (rows, 128), 1))

def leaf(block, base):
    sub, lane = iotas()
    other = 64 - base
    tiles = []
    for t in range(8):
        eye = jnp.where(lane == other + 8 * t + sub, 1.0, 0.0)
        keep = (lane >= base) & (lane < base + 64)
        tiles.append(jnp.where(keep, block[8 * t:8 * t + 8, :], eye))
    low = [None] * 8
    for g in range(8):
        c0 = base + 8 * g
        inside = (lane >= c0) & (lane < c0 + 8)
        grp = tiles[g]
        cols = [jnp.broadcast_to(grp[:, c0 + j:c0 + j + 1], (8, 128)) for j in range(8)]
        outer = {}
        for t in list(range(g + 1, 8)) + [8 + s for s in range(g)]:
            src = tiles[t] if t < 8 else low[t - 8]
            outer[t] = [jnp.broadcast_to(src[:, c0 + j:c0 + j + 1], (8, 128)) for j in range(8)]
        done = (lane >= base) & (lane < c0)
        held = grp
        grp = jnp.where(done, 0.0, grp)
        mult = jnp.zeros((8, 128), F32)
        v = jnp.where(inside, jnp.where(lane == c0 + sub, 1.0, 0.0), grp)
        scale = jnp.zeros((8, 128), F32)
        for j in range(8):
            piv = jnp.broadcast_to(cols[j][j:j + 1, :], (8, 128))
            rcp = 1.0 / piv
            m = jnp.where(sub == j, 0.0, cols[j] * rcp)
            for i in range(j + 1, 8):
                cols[i] = cols[i] - m * jnp.broadcast_to(cols[i][j:j + 1, :], (8, 128))
            mlow = jnp.where(sub > j, m, 0.0)
            grp = grp - mlow * jnp.broadcast_to(grp[j:j + 1, :], (8, 128))
            mult = jnp.where(lane == c0 + j, m, mult)
            mv = jnp.where(inside & (sub > j), 0.0, m)
            v = v - mv * jnp.broadcast_to(v[j:j + 1, :], (8, 128))
            scale = jnp.where(sub == j, rcp, scale)
        grp = jnp.where(inside & (lane < c0 + sub), mult, grp)
        tiles[g] = jnp.where(done, held, grp)
        v = v * scale
        v = jnp.where(inside, -v, v)
        rows = [jnp.broadcast_to(v[j:j + 1, :], (8, 128)) for j in range(8)]
        for t, cs in outer.items():
            src = tiles[t] if t < 8 else low[t - 8]
            p = [cs[j] * rows[j] for j in range(8)]
            tot = ((p[0] + p[1]) + (p[2] + p[3])) + ((p[4] + p[5]) + (p[6] + p[7]))
            new = jnp.where(inside, 0.0, src) - tot
            if t < 8:
                tiles[t] = new
            else:
                low[t - 8] = new
        low[g] = -v
    return jnp.concatenate(tiles, 0), jnp.concatenate(low, 0)

def lu128(blk):
    sub, lane = iotas(64)
    left = lane < 64
    z = jnp.zeros((64, 128), F32)
    top, bot = blk[:64], blk[64:]
    t0, b0 = leaf(top, 0)
    linv0 = jnp.where(left, 0.0, t0)
    uinv0 = jnp.where(left, b0, 0.0)
    u01 = jnp.where(left, 0.0, dot3(linv0, jnp.concatenate([z, top], 0)))
    l10 = dot3(jnp.where(left, bot, 0.0), jnp.concatenate([uinv0, z], 0))
    sch = bot - dot3(l10, jnp.concatenate([u01, z], 0))
    t1, b1 = leaf(sch, 64)
    linv0r = pltpu.roll(linv0, 64, 1)
    zl = dot3(l10, jnp.concatenate([linv0r, z], 0))
    zu = dot3(uinv0, jnp.concatenate([u01, z], 0))
    linv1 = jnp.where(left, t1, 0.0)
    uinv1 = jnp.where(left, 0.0, b1)
    linv10 = dot3(linv1, jnp.concatenate([zl, z], 0))
    uinv01 = dot3(zu, jnp.concatenate([z, uinv1], 0))
    packed = jnp.concatenate([jnp.where(left, t0, u01), jnp.where(left, l10, t1)], 0)
    linv = jnp.concatenate([linv0r, pltpu.roll(linv1, 64, 1) - linv10], 0)
    uinv = jnp.concatenate([uinv0 - uinv01, uinv1], 0)
    return packed, linv, uinv


def blk(i):
    return slice(TB * i, TB * (i + 1))


def later(i):
    return slice(TB * (i + 1), NB)


def pair_update(a_ref, li_ref, ui_ref, k):
    n = k + 1
    u = dot3(li_ref[k], a_ref[blk(k), blk(n)])
    l = dot3(a_ref[blk(n), blk(k)], ui_ref[k])
    a_ref[blk(k), blk(n)] = u
    a_ref[blk(n), blk(k)] = l
    a_ref[blk(n), blk(n)] = a_ref[blk(n), blk(n)] - dot3(l, u)


def half_update(a_ref, li_ref, ui_ref):
    rest = slice(HB, NB)
    u0 = dot3(li_ref[0], a_ref[blk(0), rest])
    l0 = dot3(a_ref[rest, blk(0)], ui_ref[0])
    u1 = dot3(li_ref[1], a_ref[blk(1), rest] - dot3(a_ref[blk(1), blk(0)], u0))
    l1 = dot3(a_ref[rest, blk(1)] - dot3(l0, a_ref[blk(0), blk(1)]), ui_ref[1])
    a_ref[blk(0), rest] = u0
    a_ref[blk(1), rest] = u1
    a_ref[rest, blk(0)] = l0
    a_ref[rest, blk(1)] = l1
    left = split(jnp.concatenate([l0, l1], 1))
    right = split(jnp.concatenate([u0, u1], 0))
    a_ref[rest, rest] = a_ref[rest, rest] - dot3s(left, right)


def panel_solve(a_ref, li_ref, ui_ref, q_ref, p_ref, ub_ref, lb_ref, j):
    u = dot3(li_ref[j], q_ref[blk(j), :])
    l = dot3(p_ref[:, blk(j)], ui_ref[j])
    ub_ref[blk(j), :] = u.astype(BF)
    lb_ref[:, blk(j)] = l.astype(BF)
    if j < 3:
        q_ref[later(j), :] = q_ref[later(j), :] - dot3(a_ref[later(j), blk(j)], u)
        p_ref[:, later(j)] = p_ref[:, later(j)] - dot3(l, a_ref[blk(j), later(j)])


def step_kernel(prows, pcols, remote, w_ref, o_ref, a_ref, q_ref, p_ref, li_ref, ui_ref, ub_ref, lb_ref,
                c_buf, d_buf, q_buf, p_buf, loc_sem, *sems):
    my_row = lax.axis_index("prow") if remote else 1
    my_col = lax.axis_index("pcol") if remote else 1
    hold = HB // prows
    q_hold = NB // prows
    p_hold = NB // pcols
    if remote:
        (q_send, q_recv, qs_send, qs_recv, p_send, p_recv, ps_send, ps_recv,
         c_send, c_recv, cz_send, cz_recv, ds_send, ds_recv, dz_send, dz_recv, da_send, da_recv) = sems

        def ring(axis, size, me, fn):
            def one(s, carry):
                fn(s, lax.rem(me + s, size), {axis: lax.rem(me + s, size)})
                return carry
            lax.fori_loop(1, size, one, 0)

        def rcopy(src, dst, ss, rs, dev):
            return pltpu.make_async_remote_copy(src_ref=src, dst_ref=dst, send_sem=ss, recv_sem=rs,
                                                device_id=dev, device_id_type=MESH)

        barrier = pltpu.get_barrier_semaphore()
        ring("prow", prows, my_row, lambda s, o, dev: pl.semaphore_signal(barrier, inc=1, device_id=dev, device_id_type=MESH))
        ring("pcol", pcols, my_col, lambda s, o, dev: pl.semaphore_signal(barrier, inc=1, device_id=dev, device_id_type=MESH))
        pl.semaphore_wait(barrier, prows + pcols - 2)

        def d_parts(ref, i):
            r = pl.ds(pl.multiple_of(i * hold, hold), hold)
            r2 = pl.ds(pl.multiple_of(HB + i * hold, hold), hold)
            return [ref.at[r, pl.ds(0, HB)], ref.at[r, pl.ds(HB, HB)], ref.at[r2, :]]

        def rows(ref, i, n):
            return ref.at[pl.ds(pl.multiple_of(i * n, n), n), :]

        corner = w_ref.at[pl.ds(0, TB), pl.ds(0, TB)]

        root = jnp.logical_and(my_row == 0, my_col == 0)

        @pl.when(root)
        def _():
            ring("prow", prows, my_row, lambda s, o, dev: rcopy(corner, c_buf, c_send.at[s], c_recv, dev).start())
            for part in range(3):
                ring("prow", prows, my_row, lambda s, o, dev: rcopy(
                    d_parts(w_ref, o)[part], d_parts(d_buf, o)[part], ds_send.at[part, s], ds_recv.at[part], dev).start())
            pltpu.make_async_copy(corner, c_buf, loc_sem.at[0]).start()
            for part in range(3):
                pltpu.make_async_copy(d_parts(w_ref, 0)[part], d_parts(d_buf, 0)[part], loc_sem.at[1 + part]).start()
            pltpu.make_async_copy(corner, c_buf, loc_sem.at[0]).wait()

        @pl.when(my_col == 0)
        def _():
            @pl.when(my_row != 0)
            def _():
                rcopy(corner, c_buf, c_send.at[0], c_recv, {"prow": 0}).wait_recv()
            ring("pcol", pcols, my_col, lambda s, o, dev: rcopy(c_buf, c_buf, cz_send.at[s], cz_recv, dev).start())
            for part in range(3):
                mine = d_parts(d_buf, my_row)[part]

                @pl.when(my_row == 0)
                def _():
                    pltpu.make_async_copy(d_parts(w_ref, 0)[part], mine, loc_sem.at[1 + part]).wait()

                @pl.when(my_row != 0)
                def _():
                    rcopy(mine, mine, ds_send.at[part, 0], ds_recv.at[part], {"prow": 0}).wait_recv()
                ring("pcol", pcols, my_col, lambda s, o, dev: rcopy(mine, mine, dz_send.at[part, s], dz_recv.at[part], dev).start())

        @pl.when(my_row == 0)
        def _():
            ring("prow", prows, my_row, lambda s, o, dev: rcopy(
                rows(w_ref, o, q_hold), rows(q_buf, o, q_hold), qs_send.at[s], qs_recv, dev).start())
            pltpu.make_async_copy(rows(w_ref, 0, q_hold), rows(q_buf, 0, q_hold), loc_sem.at[4]).start()

        @pl.when(my_col == 0)
        def _():
            ring("pcol", pcols, my_col, lambda s, o, dev: rcopy(
                rows(w_ref, o, p_hold), rows(p_buf, o, p_hold), ps_send.at[s], ps_recv, dev).start())
            pltpu.make_async_copy(rows(w_ref, 0, p_hold), rows(p_buf, 0, p_hold), loc_sem.at[5]).start()

        @pl.when(my_col != 0)
        def _():
            rcopy(c_buf, c_buf, cz_send.at[0], cz_recv, {"pcol": 0}).wait_recv()

    a_ref[0:TB, 0:TB] = c_buf[...].astype(F32)

    def pass_on_d():
        for part in range(3):
            mine = d_parts(d_buf, my_row)[part]

            @pl.when(my_col != 0)
            def _():
                rcopy(mine, mine, dz_send.at[part, 0], dz_recv.at[part], {"pcol": 0}).wait_recv()
            ring("prow", prows, my_row, lambda s, o, dev: rcopy(
                mine, mine, da_send.at[part, s], da_recv.at[part, my_row], dev).start())

    def pass_on_panels():
        mine_q = rows(q_buf, my_row, q_hold)
        mine_p = rows(p_buf, my_col, p_hold)

        @pl.when(my_row == 0)
        def _():
            pltpu.make_async_copy(rows(w_ref, 0, q_hold), mine_q, loc_sem.at[4]).wait()

        @pl.when(my_row != 0)
        def _():
            rcopy(mine_q, mine_q, qs_send.at[0], qs_recv, {"prow": 0}).wait_recv()

        @pl.when(my_col == 0)
        def _():
            pltpu.make_async_copy(rows(w_ref, 0, p_hold), mine_p, loc_sem.at[5]).wait()

        @pl.when(my_col != 0)
        def _():
            rcopy(mine_p, mine_p, ps_send.at[0], ps_recv, {"pcol": 0}).wait_recv()
        ring("prow", prows, my_row, lambda s, o, dev: rcopy(mine_q, mine_q, q_send.at[s], q_recv.at[my_row], dev).start())
        ring("pcol", pcols, my_col, lambda s, o, dev: rcopy(mine_p, mine_p, p_send.at[s], p_recv.at[my_col], dev).start())

    def get_d(part):
        ring("prow", prows, my_row, lambda s, o, dev: rcopy(
            d_parts(d_buf, o)[part], d_parts(d_buf, o)[part], da_send.at[part, s], da_recv.at[part, o], dev).wait_recv())

    def get_panels():
        ring("prow", prows, my_row, lambda s, o, dev: rcopy(
            rows(q_buf, o, q_hold), rows(q_buf, o, q_hold), q_send.at[s], q_recv.at[o], dev).wait_recv())
        ring("pcol", pcols, my_col, lambda s, o, dev: rcopy(
            rows(p_buf, o, p_hold), rows(p_buf, o, p_hold), p_send.at[s], p_recv.at[o], dev).wait_recv())

    def tile_step(k, carry):
        at = pl.ds(pl.multiple_of(k * TB, TB), TB)
        packed, linv, uinv = lu128(a_ref[at, at])
        a_ref[at, at] = packed
        li_ref[k] = linv
        ui_ref[k] = uinv

        @pl.when(k == 0)
        def _():
            if remote:
                pass_on_d()
                get_d(0)
            a_ref[0:TB, TB:HB] = d_buf[0:TB, TB:HB].astype(F32)
            a_ref[TB:HB, 0:HB] = d_buf[TB:HB, 0:HB].astype(F32)
            pair_update(a_ref, li_ref, ui_ref, 0)

        @pl.when(k == 1)
        def _():
            if remote:
                pass_on_panels()
                get_d(1)
                get_d(2)
            a_ref[0:HB, HB:NB] = d_buf[0:HB, HB:NB].astype(F32)
            a_ref[HB:NB, :] = d_buf[HB:NB, :].astype(F32)
            half_update(a_ref, li_ref, ui_ref)

        @pl.when(k == 2)
        def _():
            pair_update(a_ref, li_ref, ui_ref, 2)
            if remote:
                get_panels()
            q_ref[...] = q_buf[...].astype(F32)
            p_ref[...] = p_buf[...].astype(F32)
            for j in range(3):
                panel_solve(a_ref, li_ref, ui_ref, q_ref, p_ref, ub_ref, lb_ref, j)
        return carry

    lax.fori_loop(0, 4, tile_step, 0)
    panel_solve(a_ref, li_ref, ui_ref, q_ref, p_ref, ub_ref, lb_ref, 3)

    @pl.when(jnp.logical_and(my_row != 0, my_col != 0))
    def _():
        o_ref[...] = (w_ref[...].astype(F32) - dot(lb_ref[...], ub_ref[...])).astype(BF)

    @pl.when(jnp.logical_and(my_row == 0, my_col != 0))
    def _():
        o_ref[...] = ub_ref[...]

    @pl.when(jnp.logical_and(my_row != 0, my_col == 0))
    def _():
        o_ref[...] = lb_ref[...]

    @pl.when(jnp.logical_and(my_row == 0, my_col == 0))
    def _():
        o_ref[...] = a_ref[...].astype(BF)

    if remote:
        @pl.when(root)
        def _():
            ring("prow", prows, my_row, lambda s, o, dev: rcopy(corner, c_buf, c_send.at[s], c_recv, dev).wait_send())
            for part in range(3):
                ring("prow", prows, my_row, lambda s, o, dev: rcopy(
                    d_parts(w_ref, o)[part], d_parts(d_buf, o)[part], ds_send.at[part, s], ds_recv.at[part], dev).wait_send())

        @pl.when(my_col == 0)
        def _():
            ring("pcol", pcols, my_col, lambda s, o, dev: rcopy(c_buf, c_buf, cz_send.at[s], cz_recv, dev).wait_send())
            for part in range(3):
                mine = d_parts(d_buf, my_row)[part]
                ring("pcol", pcols, my_col, lambda s, o, dev: rcopy(mine, mine, dz_send.at[part, s], dz_recv.at[part], dev).wait_send())
            ring("pcol", pcols, my_col, lambda s, o, dev: rcopy(
                rows(w_ref, o, p_hold), rows(p_buf, o, p_hold), ps_send.at[s], ps_recv, dev).wait_send())

        @pl.when(my_row == 0)
        def _():
            ring("prow", prows, my_row, lambda s, o, dev: rcopy(
                rows(w_ref, o, q_hold), rows(q_buf, o, q_hold), qs_send.at[s], qs_recv, dev).wait_send())
        for part in range(3):
            mine = d_parts(d_buf, my_row)[part]
            ring("prow", prows, my_row, lambda s, o, dev: rcopy(
                mine, mine, da_send.at[part, s], da_recv.at[part, my_row], dev).wait_send())
        mine_q = rows(q_buf, my_row, q_hold)
        mine_p = rows(p_buf, my_col, p_hold)
        ring("prow", prows, my_row, lambda s, o, dev: rcopy(mine_q, mine_q, q_send.at[s], q_recv.at[my_row], dev).wait_send())
        ring("pcol", pcols, my_col, lambda s, o, dev: rcopy(mine_p, mine_p, p_send.at[s], p_recv.at[my_col], dev).wait_send())


def per_device(matrix):
    prows, pcols = lax.axis_size("prow"), lax.axis_size("pcol")
    dma = pltpu.SemaphoreType.DMA
    out = pl.pallas_call(
        functools.partial(step_kernel, prows, pcols, True),
        out_shape=jax.ShapeDtypeStruct((NB, NB), BF),
        in_specs=[pl.BlockSpec(memory_space=pltpu.VMEM)],
        out_specs=pl.BlockSpec(memory_space=pltpu.VMEM),
        scratch_shapes=[
            pltpu.VMEM((NB, NB), F32), pltpu.VMEM((NB, NB), F32), pltpu.VMEM((NB, NB), F32),
            pltpu.VMEM((4, TB, TB), F32), pltpu.VMEM((4, TB, TB), F32),
            pltpu.VMEM((NB, NB), BF), pltpu.VMEM((NB, NB), BF),
            pltpu.VMEM((TB, TB), BF), pltpu.VMEM((NB, NB), BF), pltpu.VMEM((NB, NB), BF), pltpu.VMEM((NB, NB), BF),
            dma((6,)),
            dma((prows,)), dma((prows,)), dma((prows,)), dma,
            dma((pcols,)), dma((pcols,)), dma((pcols,)), dma,
            dma((prows,)), dma, dma((pcols,)), dma,
            dma((3, prows)), dma((3,)), dma((3, pcols)), dma((3,)), dma((3, prows)), dma((3, prows)),
        ],
        compiler_params=pltpu.CompilerParams(collective_id=0, has_side_effects=True),
    )(matrix.reshape(NB, NB))
    return out.reshape(matrix.shape)


def solution(mesh):
    placed = P(None, "prow", None, "pcol")
    return jax.shard_map(per_device, mesh=mesh, in_specs=(placed,), out_specs=placed, check_vma=False)
```

time: 1300 us -> 67.7 us (0.05)
  the two profiles are of different devices: /device:TPU:40 before, /device:TPU:1 now
where the time goes in v1:
time: 67.7 us; the launch traced here: 67.5 us
  Pallas kernels  65.7 us (97%)
  local copies, waits for them, and re-layouts  1.87 us (3%)
    pallas_call x1, Pallas kernels, per_device(): pl.pallas_call(functools.partial(step_kernel, prows, pcols, True), out_sh...  65.7 us
    unnamed x1, local copies, waits for them, and re-layouts  1.87 us

profile of v1, /device:TPU:1, one launch (start us, length us, event | category | flops | bytes accessed | tf_op | source)
XLA Modules:
  0.0 67.5 jit_solution(10215963877162895792)
XLA Ops:
  0.0 65.7 %shard_map.17 = bf16[512,512]{1,0:T(8,128)(2,1)} custom-call(bf16[512,512]{1,0:T(8,128)(2,1)} %bitcast.3), custom_call_target="tpu_custom_call" | custom-call | tf_op jit(solution)/shard_map/pallas_call | solution.py:373
  65.7 1.9 %copy.3 = bf16[1,512,1,512]{3,1,2,0:T(8,128)(2,1)} copy(bf16[1,512,1,512]{3,1,2,0:T(8,128)(2,1)} %bitcast.2) | data formatting | bytes 1048576

commit v2 on v1

v2 whole, which is shorter than its diff:
```python
import functools

import jax
import jax.numpy as jnp
from jax import lax
from jax.experimental import pallas as pl
from jax.experimental.pallas import tpu as pltpu
from jax.sharding import PartitionSpec as P

F32 = jnp.float32
BF = jnp.bfloat16
NB = 512
HB = 256
TB = 128
MESH = pl.DeviceIdType.MESH


def split(x):
    hi = x.astype(BF)
    lo = (x - hi.astype(F32)).astype(BF)
    return hi, lo

def dot(a, b):
    return jnp.dot(a, b, preferred_element_type=F32)

def dot3s(a, b):
    ah, al = a; bh, bl = b
    return dot(jnp.concatenate([ah, al, ah], 1), jnp.concatenate([bh, bh, bl], 0))

def dot3(a, b):
    return dot3s(split(a), split(b))

def iotas(rows=8):
    return (lax.broadcasted_iota(jnp.int32, (rows, 128), 0), lax.broadcasted_iota(jnp.int32, (rows, 128), 1))

def leaf(block, base):
    sub, lane = iotas()
    other = 64 - base
    tiles = []
    for t in range(8):
        eye = jnp.where(lane == other + 8 * t + sub, 1.0, 0.0)
        keep = (lane >= base) & (lane < base + 64)
        tiles.append(jnp.where(keep, block[8 * t:8 * t + 8, :], eye))
    low = [None] * 8
    for g in range(8):
        c0 = base + 8 * g
        inside = (lane >= c0) & (lane < c0 + 8)
        grp = tiles[g]
        cols = [jnp.broadcast_to(grp[:, c0 + j:c0 + j + 1], (8, 128)) for j in range(8)]
        outer = {}
        for t in list(range(g + 1, 8)) + [8 + s for s in range(g)]:
            src = tiles[t] if t < 8 else low[t - 8]
            outer[t] = [jnp.broadcast_to(src[:, c0 + j:c0 + j + 1], (8, 128)) for j in range(8)]
        done = (lane >= base) & (lane < c0)
        held = grp
        grp = jnp.where(done, 0.0, grp)
        mult = jnp.zeros((8, 128), F32)
        v = jnp.where(inside, jnp.where(lane == c0 + sub, 1.0, 0.0), grp)
        scale = jnp.zeros((8, 128), F32)
        for j in range(8):
            piv = jnp.broadcast_to(cols[j][j:j + 1, :], (8, 128))
            rcp = 1.0 / piv
            m = jnp.where(sub == j, 0.0, cols[j] * rcp)
            for i in range(j + 1, 8):
                cols[i] = cols[i] - m * jnp.broadcast_to(cols[i][j:j + 1, :], (8, 128))
            mlow = jnp.where(sub > j, m, 0.0)
            grp = grp - mlow * jnp.broadcast_to(grp[j:j + 1, :], (8, 128))
            mult = jnp.where(lane == c0 + j, m, mult)
            mv = jnp.where(inside & (sub > j), 0.0, m)
            v = v - mv * jnp.broadcast_to(v[j:j + 1, :], (8, 128))
            scale = jnp.where(sub == j, rcp, scale)
        grp = jnp.where(inside & (lane < c0 + sub), mult, grp)
        tiles[g] = jnp.where(done, held, grp)
        v = v * scale
        v = jnp.where(inside, -v, v)
        rows = [jnp.broadcast_to(v[j:j + 1, :], (8, 128)) for j in range(8)]
        for t, cs in outer.items():
            src = tiles[t] if t < 8 else low[t - 8]
            p = [cs[j] * rows[j] for j in range(8)]
            tot = ((p[0] + p[1]) + (p[2] + p[3])) + ((p[4] + p[5]) + (p[6] + p[7]))
            new = jnp.where(inside, 0.0, src) - tot
            if t < 8:
                tiles[t] = new
            else:
                low[t - 8] = new
        low[g] = -v
    return jnp.concatenate(tiles, 0), jnp.concatenate(low, 0)


def second_half(t0, b0, top, bot):
    _, lane = iotas(64)
    left = lane < 64
    z = jnp.zeros((64, 128), F32)
    linv0 = jnp.where(left, 0.0, t0)
    uinv0 = jnp.where(left, b0, 0.0)
    u01 = jnp.where(left, 0.0, dot3(linv0, jnp.concatenate([z, top], 0)))
    l10 = dot3(jnp.where(left, bot, 0.0), jnp.concatenate([uinv0, z], 0))
    sch = bot - dot3(l10, jnp.concatenate([u01, z], 0))
    t1, b1 = leaf(sch, 64)
    linv0r = pltpu.roll(linv0, 64, 1)
    zl = dot3(l10, jnp.concatenate([linv0r, z], 0))
    zu = dot3(uinv0, jnp.concatenate([u01, z], 0))
    linv1 = jnp.where(left, t1, 0.0)
    uinv1 = jnp.where(left, 0.0, b1)
    linv10 = dot3(linv1, jnp.concatenate([zl, z], 0))
    uinv01 = dot3(zu, jnp.concatenate([z, uinv1], 0))
    packed = jnp.concatenate([jnp.where(left, t0, u01), jnp.where(left, l10, t1)], 0)
    linv = jnp.concatenate([linv0r, pltpu.roll(linv1, 64, 1) - linv10], 0)
    uinv = jnp.concatenate([uinv0 - uinv01, uinv1], 0)
    return packed, linv, uinv


def blk(i):
    return slice(TB * i, TB * (i + 1))


def later(i):
    return slice(TB * (i + 1), NB)


def pair_update(a_ref, li_ref, ui_ref, k):
    n = k + 1
    u = dot3(li_ref[k], a_ref[blk(k), blk(n)])
    l = dot3(a_ref[blk(n), blk(k)], ui_ref[k])
    a_ref[blk(k), blk(n)] = u
    a_ref[blk(n), blk(k)] = l
    a_ref[blk(n), blk(n)] = a_ref[blk(n), blk(n)] - dot3(l, u)


def half_update(a_ref, li_ref, ui_ref):
    rest = slice(HB, NB)
    u0 = dot3(li_ref[0], a_ref[blk(0), rest])
    l0 = dot3(a_ref[rest, blk(0)], ui_ref[0])
    u1 = dot3(li_ref[1], a_ref[blk(1), rest] - dot3(a_ref[blk(1), blk(0)], u0))
    l1 = dot3(a_ref[rest, blk(1)] - dot3(l0, a_ref[blk(0), blk(1)]), ui_ref[1])
    a_ref[blk(0), rest] = u0
    a_ref[blk(1), rest] = u1
    a_ref[rest, blk(0)] = l0
    a_ref[rest, blk(1)] = l1
    left = split(jnp.concatenate([l0, l1], 1))
    right = split(jnp.concatenate([u0, u1], 0))
    a_ref[rest, rest] = a_ref[rest, rest] - dot3s(left, right)


def solve_u(a_ref, li_ref, q_ref, ub_ref, j):
    u = dot3(li_ref[j], q_ref[blk(j), :])
    ub_ref[blk(j), :] = u.astype(BF)
    if j < 3:
        q_ref[later(j), :] = q_ref[later(j), :] - dot3(a_ref[later(j), blk(j)], u)


def solve_l(a_ref, ui_ref, p_ref, lb_ref, j):
    l = dot3(p_ref[:, blk(j)], ui_ref[j])
    lb_ref[:, blk(j)] = l.astype(BF)
    if j < 3:
        p_ref[:, later(j)] = p_ref[:, later(j)] - dot3(l, a_ref[blk(j), later(j)])


def rcopy(src, dst, ss, rs, dev):
    return pltpu.make_async_remote_copy(src_ref=src, dst_ref=dst, send_sem=ss, recv_sem=rs,
                                        device_id=dev, device_id_type=MESH)


def each(lo, hi, fn):
    def one(s, carry):
        fn(s)
        return carry
    lax.fori_loop(lo, hi, one, 0)


class Moves:
    def __init__(self, prows, pcols, w_ref, c_buf, d_buf, q_buf, p_buf, loc_sem, sems):
        self.prows, self.pcols = prows, pcols
        self.row, self.col = lax.axis_index("prow"), lax.axis_index("pcol")
        self.core = lax.rem(self.col, 2)
        self.w, self.c, self.d, self.q, self.p = w_ref, c_buf, d_buf, q_buf, p_buf
        self.loc = loc_sem
        (self.c_send, self.c_recv, self.cz_send, self.cz_recv,
         self.ds_send, self.ds_recv, self.dz_send, self.dz_recv, self.da_send, self.da_recv,
         self.qs_send, self.qs_recv, self.qa_send, self.qa_recv,
         self.ps_send, self.ps_recv, self.pa_send, self.pa_recv, self.px_send, self.px_recv) = sems
        self.root = jnp.logical_and(self.row == 0, self.col == 0)
        self.passer = self.col == jnp.where(self.row == 0, 1, 0)
        self.pass_hi = jnp.where(self.row == 0, pcols - 1, pcols)
        self.has_q = self.col != 0
        self.has_p = self.row != 0

    def up(self, s):
        return lax.rem(self.row + s, self.prows)

    def along(self, s):
        return lax.rem(self.col + s, self.pcols)

    def same_core(self, s):
        return lax.rem(self.col + 2 * s, self.pcols)

    def ready(self):
        barrier = pltpu.get_barrier_semaphore()

        def tell(dev):
            pl.semaphore_signal(barrier, inc=1, device_id=dev, device_id_type=MESH)
        each(1, self.prows, lambda s: tell({"prow": self.up(s)}))

        @pl.when(self.has_p)
        def _():
            each(1, self.pcols, lambda s: tell({"pcol": self.along(s)}))

        @pl.when(jnp.logical_and(self.row == 0, self.col == 1))
        def _():
            tell({"pcol": 0})

        @pl.when(jnp.logical_and(self.row == 0, self.col > 1))
        def _():
            tell({"pcol": 1})
        zero_row = jnp.where(self.col == 0, 1, jnp.where(self.col == 1, self.pcols - 2, 0))
        pl.semaphore_wait(barrier, self.prows - 1 + jnp.where(self.has_p, self.pcols - 1, zero_row))

    def corner(self, ref, half):
        return ref.at[pl.ds(64 * half, 64), pl.ds(0, TB)]

    def part(self, ref, i, part):
        n = HB // self.prows
        top = pl.ds(pl.multiple_of(i * n, n), n)
        low = pl.ds(pl.multiple_of(HB + i * n, n), n)
        return [ref.at[top, pl.ds(0, HB)], ref.at[top, pl.ds(HB, HB)], ref.at[low, :]][part]

    def corner_out(self, half, s):
        return rcopy(self.corner(self.w, half), self.corner(self.c, half), self.c_send.at[half, s], self.c_recv.at[half],
                     {"prow": self.up(s)})

    def corner_side(self, half):
        return rcopy(self.corner(self.w, half), self.corner(self.c, half), self.cz_send.at[half, 0], self.cz_recv.at[half],
                     {"pcol": 1})

    def corner_on(self, half, s):
        piece = self.corner(self.c, half)
        return rcopy(piece, piece, self.cz_send.at[half, s], self.cz_recv.at[half], {"pcol": self.along(s)})

    def d_out(self, part, s):
        return rcopy(self.part(self.w, self.up(s), part), self.part(self.d, self.up(s), part),
                     self.ds_send.at[part, s], self.ds_recv.at[part], {"prow": self.up(s)})

    def d_side(self, part):
        return rcopy(self.part(self.w, 0, part), self.part(self.d, 0, part),
                     self.dz_send.at[part, 0], self.dz_recv.at[part], {"pcol": 1})

    def d_on(self, part, s):
        piece = self.part(self.d, self.row, part)
        return rcopy(piece, piece, self.dz_send.at[part, s], self.dz_recv.at[part], {"pcol": self.along(s)})

    def d_share(self, part, s):
        piece = self.part(self.d, self.row, part)
        return rcopy(piece, piece, self.da_send.at[part, s], self.da_recv.at[part, self.row], {"prow": self.up(s)})

    def d_from(self, part, s):
        o = self.up(s)
        piece = self.part(self.d, o, part)
        return rcopy(piece, piece, self.da_send.at[part, s], self.da_recv.at[part, o], {"prow": o})

    def own(self, i):
        if i < 2:
            return pltpu.make_async_copy(self.corner(self.w, i), self.corner(self.c, i), self.loc.at[i])
        if i < 5:
            return pltpu.make_async_copy(self.part(self.w, 0, i - 2), self.part(self.d, 0, i - 2), self.loc.at[i])
        if i == 5:
            return pltpu.make_async_copy(self.q_piece(self.w, 0), self.q_piece(self.q, 0), self.loc.at[i])
        return pltpu.make_async_copy(self.p_piece(self.w, 0), self.p_piece(self.p, 0), self.loc.at[i])

    def q_piece(self, ref, i):
        n = NB // self.prows
        return ref.at[pl.ds(pl.multiple_of(i * n, n), n), :]

    def q_out(self, s):
        o = self.up(s)
        return rcopy(self.q_piece(self.w, o), self.q_piece(self.q, o), self.qs_send.at[s], self.qs_recv, {"prow": o})

    def q_share(self, s):
        piece = self.q_piece(self.q, self.row)
        return rcopy(piece, piece, self.qa_send.at[s], self.qa_recv.at[self.row], {"prow": self.up(s)})

    def q_from(self, s):
        o = self.up(s)
        piece = self.q_piece(self.q, o)
        return rcopy(piece, piece, self.qa_send.at[s], self.qa_recv.at[o], {"prow": o})

    def p_piece(self, ref, c):
        n = NB // self.pcols
        at = lax.rem(c, 2) * HB + (c // 2) * n
        return ref.at[pl.ds(pl.multiple_of(at, n), n), :]

    def p_half(self, h):
        return self.p.at[pl.ds(pl.multiple_of(h * HB, HB), HB), :]

    def p_out(self, s):
        o = self.along(s)
        return rcopy(self.p_piece(self.w, o), self.p_piece(self.p, o), self.ps_send.at[s], self.ps_recv, {"pcol": o})

    def p_share(self, s):
        piece = self.p_piece(self.p, self.col)
        return rcopy(piece, piece, self.pa_send.at[s], self.pa_recv.at[self.col // 2], {"pcol": self.same_core(s)})

    def p_from(self, s):
        o = self.same_core(s)
        piece = self.p_piece(self.p, o)
        return rcopy(piece, piece, self.pa_send.at[s], self.pa_recv.at[o // 2], {"pcol": o})

    def p_swap(self):
        mine = self.p_half(self.core)
        return rcopy(mine, mine, self.px_send, self.px_recv, {"pcol": self.col + 1 - 2 * self.core})

    def p_swapped(self):
        other = self.p_half(1 - self.core)
        return rcopy(other, other, self.px_send, self.px_recv, {"pcol": self.col + 1 - 2 * self.core})

    def start(self):
        self.ready()

        @pl.when(self.root)
        def _():
            for half in range(2):
                each(1, self.prows, lambda s: self.corner_out(half, s).start())
                self.corner_side(half).start()
                self.own(half).start()
            for part in range(3):
                each(1, self.prows, lambda s: self.d_out(part, s).start())
                self.d_side(part).start()
                self.own(2 + part).start()

        @pl.when(jnp.logical_and(self.row == 0, self.col > 1))
        def _():
            self.send_q()

        @pl.when(self.passer)
        def _():
            for half in range(2):
                @pl.when(self.has_p)
                def _():
                    self.corner_out(half, 0).wait_recv()

                @pl.when(jnp.logical_not(self.has_p))
                def _():
                    self.corner_side(half).wait_recv()
                each(1, self.pass_hi, lambda s: self.corner_on(half, s).start())
            for part in range(3):
                @pl.when(self.has_p)
                def _():
                    self.d_out(part, 0).wait_recv()

                @pl.when(jnp.logical_not(self.has_p))
                def _():
                    self.d_side(part).wait_recv()
                each(1, self.pass_hi, lambda s: self.d_on(part, s).start())

            @pl.when(self.has_p)
            def _():
                each(1, self.pcols, lambda s: self.p_out(s).start())
                self.own(6).start()

            @pl.when(jnp.logical_not(self.has_p))
            def _():
                self.send_q()

    def send_q(self):
        each(1, self.prows, lambda s: self.q_out(s).start())
        self.own(5).start()

    def wait_corner(self, half):
        @pl.when(self.root)
        def _():
            self.own(half).wait()

        @pl.when(jnp.logical_not(jnp.logical_or(self.root, self.passer)))
        def _():
            self.corner_on(half, 0).wait_recv()

    def share_d(self, parts):
        for part in parts:
            @pl.when(self.root)
            def _():
                self.own(2 + part).wait()

            @pl.when(jnp.logical_not(jnp.logical_or(self.root, self.passer)))
            def _():
                self.d_on(part, 0).wait_recv()
            each(1, self.prows, lambda s: self.d_share(part, s).start())

    def get_d(self, part):
        each(1, self.prows, lambda s: self.d_from(part, s).wait_recv())

    def share_q(self):
        @pl.when(self.has_q)
        def _():
            @pl.when(self.row == 0)
            def _():
                self.own(5).wait()

            @pl.when(self.row != 0)
            def _():
                self.q_out(0).wait_recv()
            each(1, self.prows, lambda s: self.q_share(s).start())

    def get_q(self):
        each(1, self.prows, lambda s: self.q_from(s).wait_recv())

    def share_p(self):
        @pl.when(self.has_p)
        def _():
            @pl.when(self.col == 0)
            def _():
                self.own(6).wait()

            @pl.when(self.col != 0)
            def _():
                self.p_out(0).wait_recv()
            each(1, self.pcols // 2, lambda s: self.p_share(s).start())

    def swap_p(self):
        @pl.when(self.has_p)
        def _():
            each(1, self.pcols // 2, lambda s: self.p_from(s).wait_recv())
            self.p_swap().start()

    def get_p(self):
        self.p_swapped().wait_recv()

    def finish(self):
        @pl.when(self.root)
        def _():
            for half in range(2):
                each(1, self.prows, lambda s: self.corner_out(half, s).wait_send())
                self.corner_side(half).wait_send()
            for part in range(3):
                each(1, self.prows, lambda s: self.d_out(part, s).wait_send())
                self.d_side(part).wait_send()

        @pl.when(self.passer)
        def _():
            for half in range(2):
                each(1, self.pass_hi, lambda s: self.corner_on(half, s).wait_send())
            for part in range(3):
                each(1, self.pass_hi, lambda s: self.d_on(part, s).wait_send())

            @pl.when(self.has_p)
            def _():
                each(1, self.pcols, lambda s: self.p_out(s).wait_send())
        for part in range(3):
            each(1, self.prows, lambda s: self.d_share(part, s).wait_send())

        @pl.when(self.has_q)
        def _():
            @pl.when(self.row == 0)
            def _():
                each(1, self.prows, lambda s: self.q_out(s).wait_send())
            each(1, self.prows, lambda s: self.q_share(s).wait_send())

        @pl.when(self.has_p)
        def _():
            each(1, self.pcols // 2, lambda s: self.p_share(s).wait_send())
            self.p_swap().wait_send()


def step_kernel(prows, pcols, w_ref, o_ref, a_ref, q_ref, p_ref, li_ref, ui_ref, ub_ref, lb_ref,
                c_buf, d_buf, q_buf, p_buf, loc_sem, *sems):
    mv = Moves(prows, pcols, w_ref, c_buf, d_buf, q_buf, p_buf, loc_sem, sems)
    mv.start()
    mv.wait_corner(0)
    a_ref[0:64, 0:TB] = c_buf[0:64, :].astype(F32)

    def tile_step(k, carry):
        at = pl.ds(pl.multiple_of(k * TB, TB), TB)
        upper = pl.ds(pl.multiple_of(k * TB, 64), 64)
        lower = pl.ds(pl.multiple_of(k * TB + 64, 64), 64)
        top = a_ref[upper, at]
        t0, b0 = leaf(top, 0)

        @pl.when(k == 0)
        def _():
            mv.wait_corner(1)
            a_ref[64:TB, 0:TB] = c_buf[64:TB, :].astype(F32)
            mv.share_d([0, 1, 2])

        @pl.when(k == 1)
        def _():
            mv.share_q()

        @pl.when(k == 3)
        def _():
            @pl.when(mv.has_q)
            def _():
                mv.get_q()
                q_ref[...] = q_buf[...].astype(F32)
                for j in range(3):
                    solve_u(a_ref, li_ref, q_ref, ub_ref, j)

            @pl.when(mv.has_p)
            def _():
                mv.get_p()
                p_ref[...] = p_buf[...].astype(F32)
                for j in range(3):
                    solve_l(a_ref, ui_ref, p_ref, lb_ref, j)

        packed, linv, uinv = second_half(t0, b0, top, a_ref[lower, at])
        a_ref[at, at] = packed
        li_ref[k] = linv
        ui_ref[k] = uinv

        @pl.when(k == 0)
        def _():
            mv.share_p()
            mv.get_d(0)
            a_ref[0:TB, TB:HB] = d_buf[0:TB, TB:HB].astype(F32)
            a_ref[TB:HB, 0:HB] = d_buf[TB:HB, 0:HB].astype(F32)
            pair_update(a_ref, li_ref, ui_ref, 0)

        @pl.when(k == 1)
        def _():
            mv.get_d(1)
            mv.get_d(2)
            a_ref[0:HB, HB:NB] = d_buf[0:HB, HB:NB].astype(F32)
            a_ref[HB:NB, :] = d_buf[HB:NB, :].astype(F32)
            half_update(a_ref, li_ref, ui_ref)

        @pl.when(k == 2)
        def _():
            pair_update(a_ref, li_ref, ui_ref, 2)
            mv.swap_p()
        return carry

    lax.fori_loop(0, 4, tile_step, 0)

    @pl.when(mv.has_q)
    def _():
        solve_u(a_ref, li_ref, q_ref, ub_ref, 3)

    @pl.when(mv.has_p)
    def _():
        solve_l(a_ref, ui_ref, p_ref, lb_ref, 3)

    @pl.when(jnp.logical_and(mv.has_p, mv.has_q))
    def _():
        o_ref[...] = (w_ref[...].astype(F32) - dot(lb_ref[...], ub_ref[...])).astype(BF)

    @pl.when(jnp.logical_and(jnp.logical_not(mv.has_p), mv.has_q))
    def _():
        o_ref[...] = ub_ref[...]

    @pl.when(jnp.logical_and(mv.has_p, jnp.logical_not(mv.has_q)))
    def _():
        o_ref[...] = lb_ref[...]

    @pl.when(mv.root)
    def _():
        o_ref[...] = a_ref[...].astype(BF)

    mv.finish()


def per_device(matrix):
    prows, pcols = lax.axis_size("prow"), lax.axis_size("pcol")
    dma = pltpu.SemaphoreType.DMA
    out = pl.pallas_call(
        functools.partial(step_kernel, prows, pcols),
        out_shape=jax.ShapeDtypeStruct((NB, NB), BF),
        in_specs=[pl.BlockSpec(memory_space=pltpu.VMEM)],
        out_specs=pl.BlockSpec(memory_space=pltpu.VMEM),
        scratch_shapes=[
            pltpu.VMEM((NB, NB), F32), pltpu.VMEM((NB, NB), F32), pltpu.VMEM((NB, NB), F32),
            pltpu.VMEM((4, TB, TB), F32), pltpu.VMEM((4, TB, TB), F32),
            pltpu.VMEM((NB, NB), BF), pltpu.VMEM((NB, NB), BF),
            pltpu.VMEM((TB, TB), BF), pltpu.VMEM((NB, NB), BF), pltpu.VMEM((NB, NB), BF), pltpu.VMEM((NB, NB), BF),
            dma((7,)),
            dma((2, prows)), dma((2,)), dma((2, pcols)), dma((2,)),
            dma((3, prows)), dma((3,)), dma((3, pcols)), dma((3,)), dma((3, prows)), dma((3, prows)),
            dma((prows,)), dma, dma((prows,)), dma((prows,)),
            dma((pcols,)), dma, dma((pcols // 2,)), dma((pcols // 2,)), dma, dma,
        ],
        compiler_params=pltpu.CompilerParams(collective_id=0, has_side_effects=True),
    )(matrix.reshape(NB, NB))
    return out.reshape(matrix.shape)


def solution(mesh):
    placed = P(None, "prow", None, "pcol")
    return jax.shard_map(per_device, mesh=mesh, in_specs=(placed,), out_specs=placed, check_vma=False)
```

time: 67.7 us -> 51.8 us (0.77)
  the two profiles are of different devices: /device:TPU:1 before, /device:TPU:29 now
where the time goes in v2:
time: 51.8 us; the launch traced here: 51.6 us
  Pallas kernels  49.7 us (96%)
  local copies, waits for them, and re-layouts  1.87 us (4%)
    pallas_call x1, Pallas kernels, per_device(): pl.pallas_call(functools.partial(step_kernel, prows, pcols), out_shape=ja...  49.7 us
    unnamed x1, local copies, waits for them, and re-layouts  1.87 us

profile of v2, /device:TPU:29, one launch (start us, length us, event | category | flops | bytes accessed | tf_op | source)
XLA Modules:
  0.0 51.6 jit_solution(13497062354093012677)
XLA Ops:
  0.0 49.7 %shard_map.17 = bf16[512,512]{1,0:T(8,128)(2,1)} custom-call(bf16[512,512]{1,0:T(8,128)(2,1)} %bitcast.3), custom_call_target="tpu_custom_call" | custom-call | tf_op jit(solution)/shard_map/pallas_call | solution.py:561
  49.7 1.9 %copy.3 = bf16[1,512,1,512]{3,1,2,0:T(8,128)(2,1)} copy(bf16[1,512,1,512]{3,1,2,0:T(8,128)(2,1)} %bitcast.2) | data formatting | bytes 1048576

commit v3 on v2

--- a/solution.py
+++ b/solution.py
@@ -12,6 +12,8 @@
 NB = 512
 HB = 256
 TB = 128
+PARTS = 5
+OWN_Q, OWN_P = 2 + PARTS, 3 + PARTS
 MESH = pl.DeviceIdType.MESH
 
 
@@ -118,28 +120,23 @@
     return slice(TB * (i + 1), NB)
 
 
-def pair_update(a_ref, li_ref, ui_ref, k):
-    n = k + 1
-    u = dot3(li_ref[k], a_ref[blk(k), blk(n)])
-    l = dot3(a_ref[blk(n), blk(k)], ui_ref[k])
-    a_ref[blk(k), blk(n)] = u
-    a_ref[blk(n), blk(k)] = l
-    a_ref[blk(n), blk(n)] = a_ref[blk(n), blk(n)] - dot3(l, u)
-
-
-def half_update(a_ref, li_ref, ui_ref):
-    rest = slice(HB, NB)
-    u0 = dot3(li_ref[0], a_ref[blk(0), rest])
-    l0 = dot3(a_ref[rest, blk(0)], ui_ref[0])
-    u1 = dot3(li_ref[1], a_ref[blk(1), rest] - dot3(a_ref[blk(1), blk(0)], u0))
-    l1 = dot3(a_ref[rest, blk(1)] - dot3(l0, a_ref[blk(0), blk(1)]), ui_ref[1])
-    a_ref[blk(0), rest] = u0
-    a_ref[blk(1), rest] = u1
-    a_ref[rest, blk(0)] = l0
-    a_ref[rest, blk(1)] = l1
-    left = split(jnp.concatenate([l0, l1], 1))
-    right = split(jnp.concatenate([u0, u1], 0))
-    a_ref[rest, rest] = a_ref[rest, rest] - dot3s(left, right)
+def strip_update(a_ref, li_ref, ui_ref, n):
+    us, ls = [], []
+    for i in range(n):
+        u = a_ref[blk(i), blk(n)]
+        l = a_ref[blk(n), blk(i)]
+        for j in range(i):
+            u = u - dot3(a_ref[blk(i), blk(j)], us[j])
+            l = l - dot3(ls[j], a_ref[blk(j), blk(i)])
+        us.append(dot3(li_ref[i], u))
+        ls.append(dot3(l, ui_ref[i]))
+    schur = a_ref[blk(n), blk(n)]
+    for u, l in zip(us, ls):
+        schur = schur - dot3(l, u)
+    for i in range(n):
+        a_ref[blk(i), blk(n)] = us[i]
+        a_ref[blk(n), blk(i)] = ls[i]
+    a_ref[blk(n), blk(n)] = schur
 
 
 def solve_u(a_ref, li_ref, q_ref, ub_ref, j):
@@ -221,8 +218,13 @@
     def part(self, ref, i, part):
         n = HB // self.prows
         top = pl.ds(pl.multiple_of(i * n, n), n)
-        low = pl.ds(pl.multiple_of(HB + i * n, n), n)
-        return [ref.at[top, pl.ds(0, HB)], ref.at[top, pl.ds(HB, HB)], ref.at[low, :]][part]
+        low = pl.multiple_of((i // 2) * n, n)
+        side = pl.ds(pl.multiple_of(lax.rem(i, 2) * HB, HB), HB)
+        if part == 0:
+            return ref.at[top, pl.ds(0, HB)]
+        if part in (1, 3):
+            return ref.at[top, pl.ds(HB + TB * (part // 2), TB)]
+        return ref.at[pl.ds(HB + TB * (part // 2 - 1) + low, n), side]
 
     def corner_out(self, half, s):
         return rcopy(self.corner(self.w, half), self.corner(self.c, half), self.c_send.at[half, s], self.c_recv.at[half],
@@ -260,9 +262,9 @@
     def own(self, i):
         if i < 2:
             return pltpu.make_async_copy(self.corner(self.w, i), self.corner(self.c, i), self.loc.at[i])
-        if i < 5:
+        if i < 2 + PARTS:
             return pltpu.make_async_copy(self.part(self.w, 0, i - 2), self.part(self.d, 0, i - 2), self.loc.at[i])
-        if i == 5:
+        if i == OWN_Q:
             return pltpu.make_async_copy(self.q_piece(self.w, 0), self.q_piece(self.q, 0), self.loc.at[i])
         return pltpu.make_async_copy(self.p_piece(self.w, 0), self.p_piece(self.p, 0), self.loc.at[i])
 
@@ -273,6 +275,11 @@
     def q_out(self, s):
         o = self.up(s)
         return rcopy(self.q_piece(self.w, o), self.q_piece(self.q, o), self.qs_send.at[s], self.qs_recv, {"prow": o})
+
+    def q_shares(self, fn):
+        first = jnp.where(self.row == 0, self.prows, self.prows - self.row)
+        each(1, first, lambda s: fn(self.q_share(s)))
+        each(first + 1, self.prows, lambda s: fn(self.q_share(s)))
 
     def q_share(self, s):
         piece = self.q_piece(self.q, self.row)
@@ -304,6 +311,9 @@
         piece = self.p_piece(self.p, o)
         return rcopy(piece, piece, self.pa_send.at[s], self.pa_recv.at[o // 2], {"pcol": o})
 
+    def p_whole(self):
+        return rcopy(self.w, self.p, self.px_send, self.px_recv, {"pcol": 1})
+
     def p_swap(self):
         mine = self.p_half(self.core)
         return rcopy(mine, mine, self.px_send, self.px_recv, {"pcol": self.col + 1 - 2 * self.core})
@@ -313,18 +323,16 @@
         return rcopy(other, other, self.px_send, self.px_recv, {"pcol": self.col + 1 - 2 * self.core})
 
     def start(self):
-        self.ready()
-
         @pl.when(self.root)
         def _():
             for half in range(2):
+                if half == 1:
+                    self.root_part(0)
                 each(1, self.prows, lambda s: self.corner_out(half, s).start())
                 self.corner_side(half).start()
                 self.own(half).start()
-            for part in range(3):
-                each(1, self.prows, lambda s: self.d_out(part, s).start())
-                self.d_side(part).start()
-                self.own(2 + part).start()
+            for part in range(1, PARTS):
+                self.root_part(part)
 
         @pl.when(jnp.logical_and(self.row == 0, self.col > 1))
         def _():
@@ -333,6 +341,8 @@
         @pl.when(self.passer)
         def _():
             for half in range(2):
+                if half == 1:
+                    self.pass_part(0)
                 @pl.when(self.has_p)
                 def _():
                     self.corner_out(half, 0).wait_recv()
@@ -341,20 +351,33 @@
                 def _():
                     self.corner_side(half).wait_recv()
                 each(1, self.pass_hi, lambda s: self.corner_on(half, s).start())
-            for part in range(3):
-                @pl.when(self.has_p)
-                def _():
-                    self.d_out(part, 0).wait_recv()
-
-                @pl.when(jnp.logical_not(self.has_p))
-                def _():
-                    self.d_side(part).wait_recv()
-                each(1, self.pass_hi, lambda s: self.d_on(part, s).start())
+
+    def root_part(self, part):
+        each(1, self.prows, lambda s: self.d_out(part, s).start())
+        self.d_side(part).start()
+        self.own(2 + part).start()
+
+    def pass_part(self, part):
+        @pl.when(self.has_p)
+        def _():
+            self.d_out(part, 0).wait_recv()
+
+        @pl.when(jnp.logical_not(self.has_p))
+        def _():
+            self.d_side(part).wait_recv()
+        each(1, self.pass_hi, lambda s: self.d_on(part, s).start())
+
+    def pass_rest(self):
+        @pl.when(self.passer)
+        def _():
+            for part in range(1, PARTS):
+                self.pass_part(part)
 
             @pl.when(self.has_p)
             def _():
-                each(1, self.pcols, lambda s: self.p_out(s).start())
-                self.own(6).start()
+                each(2, self.pcols, lambda s: self.p_out(s).start())
+                self.own(OWN_P).start()
+                self.p_whole().start()
 
             @pl.when(jnp.logical_not(self.has_p))
             def _():
@@ -362,7 +385,7 @@
 
     def send_q(self):
         each(1, self.prows, lambda s: self.q_out(s).start())
-        self.own(5).start()
+        self.own(OWN_Q).start()
 
     def wait_corner(self, half):
         @pl.when(self.root)
@@ -392,36 +415,64 @@
         def _():
             @pl.when(self.row == 0)
             def _():
-                self.own(5).wait()
+                self.own(OWN_Q).wait()
 
             @pl.when(self.row != 0)
             def _():
                 self.q_out(0).wait_recv()
-            each(1, self.prows, lambda s: self.q_share(s).start())
-
-    def get_q(self):
-        each(1, self.prows, lambda s: self.q_from(s).wait_recv())
+            self.q_shares(lambda copy: copy.start())
+
+    def get_q(self, q_ref):
+        @pl.when(self.row == 0)
+        def _():
+            q_ref[...] = self.w[...].astype(F32)
+
+        @pl.when(self.row != 0)
+        def _():
+            each(1, self.prows, lambda s: self.q_from(s).wait_recv())
+            q_ref[...] = self.q[...].astype(F32)
 
     def share_p(self):
         @pl.when(self.has_p)
         def _():
+            @pl.when(self.col == 1)
+            def _():
+                self.p_whole().wait_recv()
+
+            @pl.when(self.col > 1)
+            def _():
+                self.p_out(0).wait_recv()
             @pl.when(self.col == 0)
             def _():
-                self.own(6).wait()
-
-            @pl.when(self.col != 0)
-            def _():
-                self.p_out(0).wait_recv()
-            each(1, self.pcols // 2, lambda s: self.p_share(s).start())
+                self.own(OWN_P).wait()
+            self.p_shares(lambda copy: copy.start())
+
+    def p_shares(self, fn):
+        chips = self.pcols // 2
+        mine = self.col // 2
+        each(1, jnp.where(mine == 0, chips, chips - mine), lambda s: fn(self.p_share(s)))
+        each(jnp.where(mine == 0, chips, chips - mine + 1), chips, lambda s: fn(self.p_share(s)))
 
     def swap_p(self):
         @pl.when(self.has_p)
         def _():
-            each(1, self.pcols // 2, lambda s: self.p_from(s).wait_recv())
-            self.p_swap().start()
-
-    def get_p(self):
-        self.p_swapped().wait_recv()
+            @pl.when(self.col > 1)
+            def _():
+                each(1, self.pcols // 2, lambda s: self.p_from(s).wait_recv())
+                self.p_swap().start()
+
+    def get_p(self, p_ref):
+        @pl.when(self.col == 0)
+        def _():
+            p_ref[...] = self.w[...].astype(F32)
+
+        @pl.when(self.col > 1)
+        def _():
+            self.p_swapped().wait_recv()
+
+        @pl.when(self.col != 0)
+        def _():
+            p_ref[...] = self.p[...].astype(F32)
 
     def finish(self):
         @pl.when(self.root)
@@ -429,7 +480,7 @@
             for half in range(2):
                 each(1, self.prows, lambda s: self.corner_out(half, s).wait_send())
                 self.corner_side(half).wait_send()
-            for part in range(3):
+            for part in range(PARTS):
                 each(1, self.prows, lambda s: self.d_out(part, s).wait_send())
                 self.d_side(part).wait_send()
 
@@ -437,13 +488,13 @@
         def _():
             for half in range(2):
                 each(1, self.pass_hi, lambda s: self.corner_on(half, s).wait_send())
-            for part in range(3):
+            for part in range(PARTS):
                 each(1, self.pass_hi, lambda s: self.d_on(part, s).wait_send())
 
             @pl.when(self.has_p)
             def _():
-                each(1, self.pcols, lambda s: self.p_out(s).wait_send())
-        for part in range(3):
+                each(2, self.pcols, lambda s: self.p_out(s).wait_send())
+        for part in range(PARTS):
             each(1, self.prows, lambda s: self.d_share(part, s).wait_send())
 
         @pl.when(self.has_q)
@@ -451,17 +502,28 @@
             @pl.when(self.row == 0)
             def _():
                 each(1, self.prows, lambda s: self.q_out(s).wait_send())
-            each(1, self.prows, lambda s: self.q_share(s).wait_send())
+            self.q_shares(lambda copy: copy.wait_send())
 
         @pl.when(self.has_p)
         def _():
-            each(1, self.pcols // 2, lambda s: self.p_share(s).wait_send())
-            self.p_swap().wait_send()
-
-
-def step_kernel(prows, pcols, w_ref, o_ref, a_ref, q_ref, p_ref, li_ref, ui_ref, ub_ref, lb_ref,
+            self.p_shares(lambda copy: copy.wait_send())
+
+            @pl.when(self.col == 0)
+            def _():
+                self.p_whole().wait_send()
+
+            @pl.when(self.col > 1)
+            def _():
+                self.p_swap().wait_send()
+
+
+def step_kernel(prows, pcols, w_hbm, o_ref, w_ref, a_ref, q_ref, p_ref, li_ref, ui_ref, ub_ref, lb_ref,
                 c_buf, d_buf, q_buf, p_buf, loc_sem, *sems):
     mv = Moves(prows, pcols, w_ref, c_buf, d_buf, q_buf, p_buf, loc_sem, sems)
+    load = pltpu.make_async_copy(w_hbm, w_ref, loc_sem.at[OWN_P + 1])
+    load.start()
+    mv.ready()
+    load.wait()
     mv.start()
     mv.wait_corner(0)
     a_ref[0:64, 0:TB] = c_buf[0:64, :].astype(F32)
@@ -475,27 +537,27 @@
 
         @pl.when(k == 0)
         def _():
+            mv.share_d([0])
             mv.wait_corner(1)
             a_ref[64:TB, 0:TB] = c_buf[64:TB, :].astype(F32)
-            mv.share_d([0, 1, 2])
+            mv.pass_rest()
 
         @pl.when(k == 1)
         def _():
-            mv.share_q()
+            mv.share_d([3, 4])
+            mv.share_p()
 
         @pl.when(k == 3)
         def _():
             @pl.when(mv.has_q)
             def _():
-                mv.get_q()
-                q_ref[...] = q_buf[...].astype(F32)
+                mv.get_q(q_ref)
                 for j in range(3):
                     solve_u(a_ref, li_ref, q_ref, ub_ref, j)
 
             @pl.when(mv.has_p)
             def _():
-                mv.get_p()
-                p_ref[...] = p_buf[...].astype(F32)
+                mv.get_p(p_ref)
                 for j in range(3):
                     solve_l(a_ref, ui_ref, p_ref, lb_ref, j)
 
@@ -506,24 +568,29 @@
 
         @pl.when(k == 0)
         def _():
-            mv.share_p()
+            mv.share_d([1, 2])
             mv.get_d(0)
             a_ref[0:TB, TB:HB] = d_buf[0:TB, TB:HB].astype(F32)
             a_ref[TB:HB, 0:HB] = d_buf[TB:HB, 0:HB].astype(F32)
-            pair_update(a_ref, li_ref, ui_ref, 0)
+            strip_update(a_ref, li_ref, ui_ref, 1)
 
         @pl.when(k == 1)
         def _():
+            mv.share_q()
             mv.get_d(1)
             mv.get_d(2)
-            a_ref[0:HB, HB:NB] = d_buf[0:HB, HB:NB].astype(F32)
-            a_ref[HB:NB, :] = d_buf[HB:NB, :].astype(F32)
-            half_update(a_ref, li_ref, ui_ref)
+            a_ref[0:HB, HB:HB + TB] = d_buf[0:HB, HB:HB + TB].astype(F32)
+            a_ref[HB:HB + TB, 0:HB + TB] = d_buf[HB:HB + TB, 0:HB + TB].astype(F32)
+            strip_update(a_ref, li_ref, ui_ref, 2)
 
         @pl.when(k == 2)
         def _():
-            pair_update(a_ref, li_ref, ui_ref, 2)
             mv.swap_p()
+            mv.get_d(3)
+            mv.get_d(4)
+            a_ref[0:HB + TB, HB + TB:NB] = d_buf[0:HB + TB, HB + TB:NB].astype(F32)
+            a_ref[HB + TB:NB, :] = d_buf[HB + TB:NB, :].astype(F32)
+            strip_update(a_ref, li_ref, ui_ref, 3)
         return carry
 
     lax.fori_loop(0, 4, tile_step, 0)
@@ -560,17 +627,18 @@
     dma = pltpu.SemaphoreType.DMA
     out = pl.pallas_call(
         functools.partial(step_kernel, prows, pcols),
-        out_shape=jax.ShapeDtypeStruct((NB, NB), BF),
-        in_specs=[pl.BlockSpec(memory_space=pltpu.VMEM)],
+        out_shape=pltpu.VMEM((NB, NB), BF),
+        in_specs=[pl.BlockSpec(memory_space=pl.ANY)],
         out_specs=pl.BlockSpec(memory_space=pltpu.VMEM),
         scratch_shapes=[
+            pltpu.VMEM((NB, NB), BF),
             pltpu.VMEM((NB, NB), F32), pltpu.VMEM((NB, NB), F32), pltpu.VMEM((NB, NB), F32),
             pltpu.VMEM((4, TB, TB), F32), pltpu.VMEM((4, TB, TB), F32),
             pltpu.VMEM((NB, NB), BF), pltpu.VMEM((NB, NB), BF),
             pltpu.VMEM((TB, TB), BF), pltpu.VMEM((NB, NB), BF), pltpu.VMEM((NB, NB), BF), pltpu.VMEM((NB, NB), BF),
-            dma((7,)),
+            dma((5 + PARTS,)),
             dma((2, prows)), dma((2,)), dma((2, pcols)), dma((2,)),
-            dma((3, prows)), dma((3,)), dma((3, pcols)), dma((3,)), dma((3, prows)), dma((3, prows)),
+            dma((PARTS, prows)), dma((PARTS,)), dma((PARTS, pcols)), dma((PARTS,)), dma((PARTS, prows)), dma((PARTS, prows)),
             dma((prows,)), dma, dma((prows,)), dma((prows,)),
             dma((pcols,)), dma, dma((pcols // 2,)), dma((pcols // 2,)), dma, dma,
         ],

time: 51.8 us -> 46.1 us (0.89)
  the two profiles are of different devices: /device:TPU:29 before, /device:TPU:40 now
where the time goes in v3:
time: 46.1 us; the launch traced here: 46 us
  Pallas kernels  45.2 us (98%)
  local copies, waits for them, and re-layouts  0.8 us (2%)
    pallas_call x1, Pallas kernels, per_device(): pl.pallas_call(functools.partial(step_kernel, prows, pcols), out_shape=pl...  45.2 us

profile of v3, /device:TPU:40, one launch (start us, length us, event | category | flops | bytes accessed | tf_op | source)
XLA Modules:
  0.0 46.0 jit_solution(11103489017541285963)
XLA Ops:
  0.0 45.2 %shard_map.17 = bf16[512,512]{1,0:T(8,128)(2,1)S(1)} custom-call(bf16[512,512]{1,0:T(8,128)(2,1)} %bitcast.3), custom_call_target="tpu_custom_call" | custom-call | tf_op jit(solution)/shard_map/pallas_call | solution.py:628
  45.2 0.8 %copy.3 = bf16[1,512,1,512]{3,1,2,0:T(8,128)(2,1)} copy(bf16[1,512,1,512]{3,1,2,0:T(8,128)(2,1)S(1)} %bitcast.2) | data formatting | bytes 1048576

commit v4 on v3

--- a/solution.py
+++ b/solution.py
@@ -325,9 +325,8 @@
     def start(self):
         @pl.when(self.root)
         def _():
+            self.root_part(0)
             for half in range(2):
-                if half == 1:
-                    self.root_part(0)
                 each(1, self.prows, lambda s: self.corner_out(half, s).start())
                 self.corner_side(half).start()
                 self.own(half).start()
@@ -340,9 +339,8 @@
 
         @pl.when(self.passer)
         def _():
+            self.pass_part(0)
             for half in range(2):
-                if half == 1:
-                    self.pass_part(0)
                 @pl.when(self.has_p)
                 def _():
                     self.corner_out(half, 0).wait_recv()
@@ -525,6 +523,7 @@
     mv.ready()
     load.wait()
     mv.start()
+    mv.share_d([0])
     mv.wait_corner(0)
     a_ref[0:64, 0:TB] = c_buf[0:64, :].astype(F32)
 
@@ -537,7 +536,6 @@
 
         @pl.when(k == 0)
         def _():
-            mv.share_d([0])
             mv.wait_corner(1)
             a_ref[64:TB, 0:TB] = c_buf[64:TB, :].astype(F32)
             mv.pass_rest()
@@ -585,9 +583,9 @@
 
         @pl.when(k == 2)
         def _():
-            mv.swap_p()
             mv.get_d(3)
             mv.get_d(4)
+            mv.swap_p()
             a_ref[0:HB + TB, HB + TB:NB] = d_buf[0:HB + TB, HB + TB:NB].astype(F32)
             a_ref[HB + TB:NB, :] = d_buf[HB + TB:NB, :].astype(F32)
             strip_update(a_ref, li_ref, ui_ref, 3)

time: 46.1 us -> 44.6 us (0.967)
  Pallas kernels: 45.2 us -> 43.5 us
    pallas_call x1, Pallas kernels: 45.2 us -> 43.5 us  [per_device(): pl.pallas_call(functools.partial(step_kernel, prows, pcols), out_shape=pl...]
where the time goes in v4:
time: 44.6 us; the launch traced here: 44.3 us
  Pallas kernels  43.5 us (98%)
  local copies, waits for them, and re-layouts  0.8 us (2%)
    pallas_call x1, Pallas kernels, per_device(): pl.pallas_call(functools.partial(step_kernel, prows, pcols), out_shape=pl...  43.5 us

profile of v4, /device:TPU:40, one launch (start us, length us, event | category | flops | bytes accessed | tf_op | source)
XLA Modules:
  0.0 44.3 jit_solution(1451049830251577937)
XLA Ops:
  0.0 43.5 %shard_map.17 = bf16[512,512]{1,0:T(8,128)(2,1)S(1)} custom-call(bf16[512,512]{1,0:T(8,128)(2,1)} %bitcast.3), custom_call_target="tpu_custom_call" | custom-call | tf_op jit(solution)/shard_map/pallas_call | solution.py:626
  43.5 0.8 %copy.3 = bf16[1,512,1,512]{3,1,2,0:T(8,128)(2,1)} copy(bf16[1,512,1,512]{3,1,2,0:T(8,128)(2,1)S(1)} %bitcast.2) | data formatting | bytes 1048576

commit v5 on v4

--- a/solution.py
+++ b/solution.py
@@ -365,16 +365,25 @@
             self.d_side(part).wait_recv()
         each(1, self.pass_hi, lambda s: self.d_on(part, s).start())
 
+    def pass_next(self):
+        @pl.when(self.passer)
+        def _():
+            for part in range(1, 3):
+                self.pass_part(part)
+
+            @pl.when(self.has_p)
+            def _():
+                each(2, self.pcols, lambda s: self.p_out(s).start())
+                self.own(OWN_P).start()
+
     def pass_rest(self):
         @pl.when(self.passer)
         def _():
-            for part in range(1, PARTS):
+            for part in range(3, PARTS):
                 self.pass_part(part)
 
             @pl.when(self.has_p)
             def _():
-                each(2, self.pcols, lambda s: self.p_out(s).start())
-                self.own(OWN_P).start()
                 self.p_whole().start()
 
             @pl.when(jnp.logical_not(self.has_p))
@@ -538,26 +547,13 @@
         def _():
             mv.wait_corner(1)
             a_ref[64:TB, 0:TB] = c_buf[64:TB, :].astype(F32)
-            mv.pass_rest()
+            mv.pass_next()
 
         @pl.when(k == 1)
         def _():
             mv.share_d([3, 4])
+            mv.share_q()
             mv.share_p()
-
-        @pl.when(k == 3)
-        def _():
-            @pl.when(mv.has_q)
-            def _():
-                mv.get_q(q_ref)
-                for j in range(3):
-                    solve_u(a_ref, li_ref, q_ref, ub_ref, j)
-
-            @pl.when(mv.has_p)
-            def _():
-                mv.get_p(p_ref)
-                for j in range(3):
-                    solve_l(a_ref, ui_ref, p_ref, lb_ref, j)
 
         packed, linv, uinv = second_half(t0, b0, top, a_ref[lower, at])
         a_ref[at, at] = packed
@@ -566,6 +562,7 @@
 
         @pl.when(k == 0)
         def _():
+            mv.pass_rest()
             mv.share_d([1, 2])
             mv.get_d(0)
             a_ref[0:TB, TB:HB] = d_buf[0:TB, TB:HB].astype(F32)
@@ -574,7 +571,6 @@
 
         @pl.when(k == 1)
         def _():
-            mv.share_q()
             mv.get_d(1)
             mv.get_d(2)
             a_ref[0:HB, HB:HB + TB] = d_buf[0:HB, HB:HB + TB].astype(F32)
@@ -595,22 +591,29 @@
 
     @pl.when(mv.has_q)
     def _():
-        solve_u(a_ref, li_ref, q_ref, ub_ref, 3)
+        mv.get_q(q_ref)
 
     @pl.when(mv.has_p)
     def _():
-        solve_l(a_ref, ui_ref, p_ref, lb_ref, 3)
+        mv.get_p(p_ref)
 
     @pl.when(jnp.logical_and(mv.has_p, mv.has_q))
     def _():
+        for j in range(4):
+            solve_u(a_ref, li_ref, q_ref, ub_ref, j)
+            solve_l(a_ref, ui_ref, p_ref, lb_ref, j)
         o_ref[...] = (w_ref[...].astype(F32) - dot(lb_ref[...], ub_ref[...])).astype(BF)
 
     @pl.when(jnp.logical_and(jnp.logical_not(mv.has_p), mv.has_q))
     def _():
+        for j in range(4):
+            solve_u(a_ref, li_ref, q_ref, ub_ref, j)
         o_ref[...] = ub_ref[...]
 
     @pl.when(jnp.logical_and(mv.has_p, jnp.logical_not(mv.has_q)))
     def _():
+        for j in range(4):
+            solve_l(a_ref, ui_ref, p_ref, lb_ref, j)
         o_ref[...] = lb_ref[...]
 
     @pl.when(mv.root)

time: 44.6 us -> 43.5 us (0.975)
  Pallas kernels: 43.5 us -> 42.1 us
    pallas_call x1, Pallas kernels: 43.5 us -> 42.1 us  [per_device(): pl.pallas_call(functools.partial(step_kernel, prows, pcols), out_shape=pl...]
where the time goes in v5:
time: 43.5 us; the launch traced here: 42.9 us
  Pallas kernels  42.1 us (97%)
  local copies, waits for them, and re-layouts  0.8 us (2%)
    pallas_call x1, Pallas kernels, per_device(): pl.pallas_call(functools.partial(step_kernel, prows, pcols), out_shape=pl...  42.1 us

profile of v5, /device:TPU:40, one launch (start us, length us, event | category | flops | bytes accessed | tf_op | source)
XLA Modules:
  0.0 42.9 jit_solution(11767007822125632953)
XLA Ops:
  0.0 42.1 %shard_map.17 = bf16[512,512]{1,0:T(8,128)(2,1)S(1)} custom-call(bf16[512,512]{1,0:T(8,128)(2,1)} %bitcast.3), custom_call_target="tpu_custom_call" | custom-call | tf_op jit(solution)/shard_map/pallas_call | solution.py:629
  42.1 0.8 %copy.3 = bf16[1,512,1,512]{3,1,2,0:T(8,128)(2,1)} copy(bf16[1,512,1,512]{3,1,2,0:T(8,128)(2,1)S(1)} %bitcast.2) | data formatting | bytes 1048576

commit v6 on v5

--- a/solution.py
+++ b/solution.py
@@ -183,7 +183,7 @@
         self.has_p = self.row != 0
 
     def up(self, s):
-        return lax.rem(self.row + s, self.prows)
+        return lax.rem(self.row + jnp.where(self.core == 0, s, self.prows - s), self.prows)
 
     def along(self, s):
         return lax.rem(self.col + s, self.pcols)
@@ -277,7 +277,7 @@
         return rcopy(self.q_piece(self.w, o), self.q_piece(self.q, o), self.qs_send.at[s], self.qs_recv, {"prow": o})
 
     def q_shares(self, fn):
-        first = jnp.where(self.row == 0, self.prows, self.prows - self.row)
+        first = jnp.where(self.row == 0, self.prows, jnp.where(self.core == 0, self.prows - self.row, self.row))
         each(1, first, lambda s: fn(self.q_share(s)))
         each(first + 1, self.prows, lambda s: fn(self.q_share(s)))
 

time: 43.5 us -> 43.7 us (level)
  no operation moved by 1% of the time
where the time goes in v6:
time: 43.7 us; the launch traced here: 42.8 us
  Pallas kernels  42 us (96%)
  local copies, waits for them, and re-layouts  0.8 us (2%)
    pallas_call x1, Pallas kernels, per_device(): pl.pallas_call(functools.partial(step_kernel, prows, pcols), out_shape=pl...  42 us

profile of v6, /device:TPU:40, one launch (start us, length us, event | category | flops | bytes accessed | tf_op | source)
XLA Modules:
  0.0 42.8 jit_solution(11886782945355255473)
XLA Ops:
  0.0 42.0 %shard_map.17 = bf16[512,512]{1,0:T(8,128)(2,1)S(1)} custom-call(bf16[512,512]{1,0:T(8,128)(2,1)} %bitcast.3), custom_call_target="tpu_custom_call" | custom-call | tf_op jit(solution)/shard_map/pallas_call | solution.py:629
  42.0 0.8 %copy.3 = bf16[1,512,1,512]{3,1,2,0:T(8,128)(2,1)} copy(bf16[1,512,1,512]{3,1,2,0:T(8,128)(2,1)S(1)} %bitcast.2) | data formatting | bytes 1048576

commit v7 on v6

--- a/solution.py
+++ b/solution.py
@@ -189,7 +189,7 @@
         return lax.rem(self.col + s, self.pcols)
 
     def same_core(self, s):
-        return lax.rem(self.col + 2 * s, self.pcols)
+        return lax.rem(self.col + jnp.where(self.core == 0, 2 * s, self.pcols - 2 * s), self.pcols)
 
     def ready(self):
         barrier = pltpu.get_barrier_semaphore()
@@ -457,8 +457,9 @@
     def p_shares(self, fn):
         chips = self.pcols // 2
         mine = self.col // 2
-        each(1, jnp.where(mine == 0, chips, chips - mine), lambda s: fn(self.p_share(s)))
-        each(jnp.where(mine == 0, chips, chips - mine + 1), chips, lambda s: fn(self.p_share(s)))
+        skip = jnp.where(mine == 0, chips, jnp.where(self.core == 0, chips - mine, mine))
+        each(1, skip, lambda s: fn(self.p_share(s)))
+        each(skip + 1, chips, lambda s: fn(self.p_share(s)))
 
     def swap_p(self):
         @pl.when(self.has_p)

time: 43.7 us -> 44.6 us (1.021)
  the two profiles are of different devices: /device:TPU:40 before, /device:TPU:61 now
where the time goes in v7:
time: 44.6 us; the launch traced here: 44.5 us
  Pallas kernels  43.7 us (98%)
  local copies, waits for them, and re-layouts  0.8 us (2%)
    pallas_call x1, Pallas kernels, per_device(): pl.pallas_call(functools.partial(step_kernel, prows, pcols), out_shape=pl...  43.7 us

profile of v7, /device:TPU:61, one launch (start us, length us, event | category | flops | bytes accessed | tf_op | source)
XLA Modules:
  0.0 44.5 jit_solution(7207065149276621182)
XLA Ops:
  0.0 43.7 %shard_map.17 = bf16[512,512]{1,0:T(8,128)(2,1)S(1)} custom-call(bf16[512,512]{1,0:T(8,128)(2,1)} %bitcast.3), custom_call_target="tpu_custom_call" | custom-call | tf_op jit(solution)/shard_map/pallas_call | solution.py:630
  43.7 0.8 %copy.3 = bf16[1,512,1,512]{3,1,2,0:T(8,128)(2,1)} copy(bf16[1,512,1,512]{3,1,2,0:T(8,128)(2,1)S(1)} %bitcast.2) | data formatting | bytes 1048576
